TPU v7x, 32 devices: a whole 2x2x4 slice. The times are simulated.
32 devices in a mesh: fsdp: 4 (over x, core), ctx: 2 (over y), tp: 4 (over z).
Axes of the slice: x: 2, y: 2, z: 4, core: 2. Of those that a mesh axis runs over, the one named last changes fastest.
Arguments:
- tokens: bfloat16 [16, 2048, 1152], P('fsdp', ('ctx', 'tp')), may hold values from -6 to 6
- picture: int32 [16, 2048], P('fsdp', 'ctx'), may hold values from 0 to 3, never falling along the last dimension, each value on 1 to 1024 neighbouring positions
- ln1_gain: float32 [1152], replicated, may hold values from 0.5 to 1.5
- ln1_bias: float32 [1152], replicated, may hold values from -1 to 1
- w_query: bfloat16 [1152, 1152], P('fsdp', 'tp'), may hold values from -0.1875 to 0.1875
- b_query: float32 [1152], replicated, may hold values from -1 to 1
- w_key: bfloat16 [1152, 1152], P('fsdp', 'tp'), may hold values from -0.1875 to 0.1875
- w_value: bfloat16 [1152, 1152], P('fsdp', 'tp'), may hold values from -0.1875 to 0.1875
- b_value: float32 [1152], replicated, may hold values from -1 to 1
- w_output: bfloat16 [1152, 1152], P('tp', 'fsdp'), may hold values from -4 to 4
- b_output: float32 [1152], replicated, may hold values from -1 to 1
- ln2_gain: float32 [1152], replicated, may hold values from 0.5 to 1.5
- ln2_bias: float32 [1152], replicated, may hold values from -1 to 1
- w_first: bfloat16 [1152, 4304], P('fsdp', 'tp'), may hold values from -0.1875 to 0.1875
- b_first: float32 [4304], replicated, may hold values from -1 to 1
- w_second: bfloat16 [4304, 1152], P('tp', 'fsdp'), may hold values from -0.09375 to 0.09375
- b_second: float32 [1152], replicated, may hold values from -1 to 1
- cotangent: bfloat16 [16, 2048, 1152], P('fsdp', ('ctx', 'tp')), may hold values from -6 to 6
Outputs:
- output: bfloat16 [16, 2048, 1152], P('fsdp', ('ctx', 'tp'))
- grad_tokens: float32 [16, 2048, 1152], P('fsdp', ('ctx', 'tp'))
- grad_ln1_gain: float32 [1152], replicated
- grad_ln1_bias: float32 [1152], replicated
- grad_w_query: float32 [1152, 1152], P(('fsdp', 'ctx'), 'tp')
- grad_b_query: float32 [1152], replicated
- grad_w_key: float32 [1152, 1152], P(('fsdp', 'ctx'), 'tp')
- grad_w_value: float32 [1152, 1152], P(('fsdp', 'ctx'), 'tp')
- grad_b_value: float32 [1152], replicated
- grad_w_output: float32 [1152, 1152], P('tp', ('fsdp', 'ctx'))
- grad_b_output: float32 [1152], replicated
- grad_ln2_gain: float32 [1152], replicated
- grad_ln2_bias: float32 [1152], replicated
- grad_w_first: float32 [1152, 4304], P(('fsdp', 'ctx'), 'tp')
- grad_b_first: float32 [4304], replicated
- grad_w_second: float32 [4304, 1152], P('tp', ('fsdp', 'ctx'))
- grad_b_second: float32 [1152], replicated
Inputs may be any that keep to these rules, and one draw needn't show every extreme that they name: In each row picture numbers never fall along the 2048 tokens; each picture holds 1 to 1024 tokens and one holds exactly 1024.
All inputs are finite; a program needn't handle non-finite values.
Results may differ from a plain program's by a relative error of at most 0.02.
Values may be sent and summed in bfloat16 or wider, within the bound.
A program may use at most 512 MiB of HBM per device.

v0:
```python
import jax
import jax.numpy as jnp
from jax import lax
from jax.sharding import PartitionSpec as P

D = 1152
HD = 72
FF = 4304
EPSILON = 1e-06


def layer_norm(values, gain, bias):
    centred = values - jnp.mean(values, axis=-1, keepdims=True)
    variance = jnp.mean(centred * centred, axis=-1, keepdims=True)
    return centred * lax.rsqrt(variance + EPSILON) * gain + bias


def matmul(left, right):
    return jnp.dot(left, right, preferred_element_type=jnp.float32)


def shards(
    tokens,
    picture,
    ln1_gain,
    ln1_bias,
    w_query,
    b_query,
    w_key,
    w_value,
    b_value,
    w_output,
    b_output,
    ln2_gain,
    ln2_bias,
    w_first,
    b_first,
    w_second,
    b_second,
    cotangent,
):
    tp_index = lax.axis_index("tp")
    wq_all, wk_all, wv_all, wo_all, wf_all, ws_all = (
        lax.all_gather(w_query, "fsdp", axis=0, tiled=True),
        lax.all_gather(w_key, "fsdp", axis=0, tiled=True),
        lax.all_gather(w_value, "fsdp", axis=0, tiled=True),
        lax.all_gather(w_output, "fsdp", axis=1, tiled=True),
        lax.all_gather(w_first, "fsdp", axis=0, tiled=True),
        lax.all_gather(w_second, "fsdp", axis=1, tiled=True),
    )
    columns = wq_all.shape[1]
    heads_dev = columns // HD
    units = wf_all.shape[1]
    bq_local = lax.dynamic_slice_in_dim(b_query, tp_index * columns, columns)
    bv_local = lax.dynamic_slice_in_dim(b_value, tp_index * columns, columns)
    first_use, second_use = (wf_all, ws_all)
    first_bias = lax.dynamic_slice_in_dim(b_first, tp_index * units, units)
    scale = HD ** (-0.5)
    grad_query = jnp.zeros(wq_all.shape, jnp.float32)
    grad_key = jnp.zeros(wk_all.shape, jnp.float32)
    grad_value = jnp.zeros(wv_all.shape, jnp.float32)
    grad_out = jnp.zeros(wo_all.shape, jnp.float32)
    grad_first = jnp.zeros(first_use.shape, jnp.float32)
    grad_second = jnp.zeros(second_use.shape, jnp.float32)
    grad_first_bias = jnp.zeros(first_bias.shape, jnp.float32)
    grad_bq = jnp.zeros((columns,), jnp.float32)
    grad_bv = jnp.zeros((columns,), jnp.float32)
    grad_bo = jnp.zeros((D,), jnp.float32)
    grad_bs = jnp.zeros((D,), jnp.float32)
    grad_g1 = jnp.zeros((D,), jnp.float32)
    grad_c1 = jnp.zeros((D,), jnp.float32)
    grad_g2 = jnp.zeros((D,), jnp.float32)
    grad_c2 = jnp.zeros((D,), jnp.float32)
    outputs = []
    input_grads = []
    for batch_index in range(tokens.shape[0]):
        row_input = tokens[batch_index].astype(jnp.float32)
        query_ids = picture[batch_index]
        row_cot = cotangent[batch_index]
        normed = layer_norm(row_input, ln1_gain, ln1_bias).astype(jnp.bfloat16)
        normed_all = lax.all_gather(normed, "tp", axis=0, tiled=True)
        half_rows = normed_all.shape[0]
        queries = (matmul(normed_all, wq_all) + bq_local).astype(jnp.bfloat16)
        keys = matmul(normed_all, wk_all).astype(jnp.bfloat16)
        values = (matmul(normed_all, wv_all) + bv_local).astype(jnp.bfloat16)
        keys_all, values_all, key_ids = (
            lax.all_gather(keys, "ctx", axis=0, tiled=True),
            lax.all_gather(values, "ctx", axis=0, tiled=True),
            lax.all_gather(query_ids, "ctx", axis=0, tiled=True),
        )
        key_rows = keys_all.shape[0]
        query_heads = queries.reshape(half_rows, heads_dev, HD)
        key_heads = keys_all.reshape(key_rows, heads_dev, HD)
        value_heads = values_all.reshape(key_rows, heads_dev, HD)
        same = (query_ids[:, None] == key_ids[None, :])[None, :, :]

        def masked_scores():
            raw = (
                jnp.einsum(
                    "qhd,khd->hqk", query_heads, key_heads, preferred_element_type=jnp.float32
                )
                * scale
            )
            return jnp.where(same, raw, -1e30)

        scores = masked_scores()
        row_max = jnp.max(scores, axis=-1, keepdims=True)
        row_total = jnp.sum(jnp.exp(scores - row_max), axis=-1, keepdims=True)
        probs_low = (jnp.exp(scores - row_max) / row_total).astype(jnp.bfloat16)
        attended = (
            jnp.einsum("hqk,khd->qhd", probs_low, value_heads, preferred_element_type=jnp.float32)
            .reshape(half_rows, columns)
            .astype(jnp.bfloat16)
        )
        hidden = (
            row_input
            + lax.psum_scatter(
                matmul(attended, wo_all).astype(jnp.bfloat16), "tp", scatter_dimension=0, tiled=True
            ).astype(jnp.float32)
            + b_output
        )
        normed_two = layer_norm(hidden, ln2_gain, ln2_bias).astype(jnp.bfloat16)
        normed_two_all, cot_all = (
            lax.all_gather(normed_two, "tp", axis=0, tiled=True),
            lax.all_gather(row_cot, "tp", axis=0, tiled=True),
        )
        before = matmul(normed_two_all, first_use) + first_bias
        active = jax.nn.gelu(before).astype(jnp.bfloat16)
        mixed = (
            lax.psum_scatter(
                matmul(active, second_use).astype(jnp.bfloat16),
                "tp",
                scatter_dimension=0,
                tiled=True,
            ).astype(jnp.float32)
            + b_second
        )
        d_active = matmul(cot_all, second_use.T)
        _, gelu_back = jax.vjp(jax.nn.gelu, before)
        d_before = gelu_back(d_active)[0].astype(jnp.bfloat16)
        grad_second = grad_second + matmul(active.T, cot_all)
        grad_first = grad_first + matmul(normed_two_all.T, d_before)
        grad_first_bias = grad_first_bias + jnp.sum(d_before.astype(jnp.float32), axis=0)
        d_normed_two = lax.psum_scatter(
            matmul(d_before, first_use.T).astype(jnp.bfloat16),
            "tp",
            scatter_dimension=0,
            tiled=True,
        ).astype(jnp.float32)
        outputs.append((hidden + mixed).astype(jnp.bfloat16))
        cot_float = row_cot.astype(jnp.float32)
        grad_bs = grad_bs + jnp.sum(cot_float, axis=0)
        _, norm_two_back = jax.vjp(layer_norm, hidden, ln2_gain, ln2_bias)
        d_hidden_norm, d_gain_two, d_bias_two = norm_two_back(d_normed_two)
        grad_g2 = grad_g2 + d_gain_two
        grad_c2 = grad_c2 + d_bias_two
        d_hidden = cot_float + d_hidden_norm
        d_attention = d_hidden.astype(jnp.bfloat16)
        grad_bo = grad_bo + jnp.sum(d_attention.astype(jnp.float32), axis=0)
        d_attention_all = lax.all_gather(d_attention, "tp", axis=0, tiled=True)
        grad_out = grad_out + matmul(attended.T, d_attention_all)
        d_attended = (
            matmul(d_attention_all, wo_all.T).astype(jnp.bfloat16).reshape(half_rows, heads_dev, HD)
        )
        scores_again = masked_scores()
        probs = jnp.exp(scores_again - row_max) / row_total
        probs_again = probs.astype(jnp.bfloat16)
        d_values_full = jnp.einsum(
            "hqk,qhd->khd", probs_again, d_attended, preferred_element_type=jnp.float32
        ).reshape(key_rows, columns)
        d_probs = jnp.einsum(
            "qhd,khd->hqk", d_attended, value_heads, preferred_element_type=jnp.float32
        )
        weighted = jnp.sum(probs * d_probs, axis=-1, keepdims=True)
        d_scores = (probs * (d_probs - weighted)).astype(jnp.bfloat16)
        d_queries = (
            (
                jnp.einsum("hqk,khd->qhd", d_scores, key_heads, preferred_element_type=jnp.float32)
                * scale
            )
            .reshape(half_rows, columns)
            .astype(jnp.bfloat16)
        )
        d_keys_full = (
            jnp.einsum("hqk,qhd->khd", d_scores, query_heads, preferred_element_type=jnp.float32)
            * scale
        ).reshape(key_rows, columns)
        d_keys_sum, d_values_sum = (
            lax.psum_scatter(
                d_keys_full.astype(jnp.bfloat16), "ctx", scatter_dimension=0, tiled=True
            ).astype(jnp.float32),
            lax.psum_scatter(
                d_values_full.astype(jnp.bfloat16), "ctx", scatter_dimension=0, tiled=True
            ).astype(jnp.float32),
        )
        d_keys = d_keys_sum.astype(jnp.bfloat16)
        d_values = d_values_sum.astype(jnp.bfloat16)
        grad_query = grad_query + matmul(normed_all.T, d_queries)
        grad_key = grad_key + matmul(normed_all.T, d_keys)
        grad_value = grad_value + matmul(normed_all.T, d_values)
        grad_bq = grad_bq + jnp.sum(d_queries.astype(jnp.float32), axis=0)
        grad_bv = grad_bv + jnp.sum(d_values.astype(jnp.float32), axis=0)
        normed_term = (
            matmul(d_queries, wq_all.T) + matmul(d_keys, wk_all.T) + matmul(d_values, wv_all.T)
        )
        d_normed = lax.psum_scatter(
            normed_term.astype(jnp.bfloat16), "tp", scatter_dimension=0, tiled=True
        ).astype(jnp.float32)
        _, norm_one_back = jax.vjp(layer_norm, row_input, ln1_gain, ln1_bias)
        d_input_norm, d_gain_one, d_bias_one = norm_one_back(d_normed)
        grad_g1 = grad_g1 + d_gain_one
        grad_c1 = grad_c1 + d_bias_one
        input_grads.append(d_hidden + d_input_norm)
    bias_first_full = lax.dynamic_update_slice(
        jnp.zeros((FF,), jnp.float32), grad_first_bias, (tp_index * units,)
    )
    grad_query, grad_key, grad_value, grad_out, grad_first, grad_second = (
        lax.psum_scatter(
            grad_query.astype(jnp.bfloat16), ("fsdp", "ctx"), scatter_dimension=0, tiled=True
        ).astype(jnp.float32),
        lax.psum_scatter(
            grad_key.astype(jnp.bfloat16), ("fsdp", "ctx"), scatter_dimension=0, tiled=True
        ).astype(jnp.float32),
        lax.psum_scatter(
            grad_value.astype(jnp.bfloat16), ("fsdp", "ctx"), scatter_dimension=0, tiled=True
        ).astype(jnp.float32),
        lax.psum_scatter(
            grad_out.astype(jnp.bfloat16), ("fsdp", "ctx"), scatter_dimension=1, tiled=True
        ).astype(jnp.float32),
        lax.psum_scatter(
            grad_first.astype(jnp.bfloat16), ("fsdp", "ctx"), scatter_dimension=0, tiled=True
        ).astype(jnp.float32),
        lax.psum_scatter(
            grad_second.astype(jnp.bfloat16), ("fsdp", "ctx"), scatter_dimension=1, tiled=True
        ).astype(jnp.float32),
    )
    bq_full = lax.dynamic_update_slice(jnp.zeros((D,), jnp.float32), grad_bq, (tp_index * columns,))
    bv_full = lax.dynamic_update_slice(jnp.zeros((D,), jnp.float32), grad_bv, (tp_index * columns,))
    grad_g1, grad_c1, bq_full, bv_full, grad_bo, grad_g2, grad_c2, bias_first_full, grad_bs = (
        lax.psum(
            (
                grad_g1,
                grad_c1,
                bq_full,
                bv_full,
                grad_bo,
                grad_g2,
                grad_c2,
                bias_first_full,
                grad_bs,
            ),
            ("fsdp", "ctx", "tp"),
        )
    )
    return (
        jnp.stack(outputs, 0),
        jnp.stack(input_grads, 0),
        grad_g1,
        grad_c1,
        grad_query,
        bq_full,
        grad_key,
        grad_value,
        bv_full,
        grad_out,
        grad_bo,
        grad_g2,
        grad_c2,
        grad_first,
        bias_first_full,
        grad_second,
        grad_bs,
    )


def solution(mesh):
    return jax.shard_map(
        shards,
        mesh=mesh,
        in_specs=(
            P("fsdp", ("ctx", "tp"), None),
            P("fsdp", "ctx"),
            P(),
            P(),
            P("fsdp", "tp"),
            P(),
            P("fsdp", "tp"),
            P("fsdp", "tp"),
            P(),
            P("tp", "fsdp"),
            P(),
            P(),
            P(),
            P("fsdp", "tp"),
            P(),
            P("tp", "fsdp"),
            P(),
            P("fsdp", ("ctx", "tp"), None),
        ),
        out_specs=(
            P("fsdp", ("ctx", "tp"), None),
            P("fsdp", ("ctx", "tp"), None),
            P(),
            P(),
            P(("fsdp", "ctx"), "tp"),
            P(),
            P(("fsdp", "ctx"), "tp"),
            P(("fsdp", "ctx"), "tp"),
            P(),
            P("tp", ("fsdp", "ctx")),
            P(),
            P(),
            P(),
            P(("fsdp", "ctx"), "tp"),
            P(),
            P("tp", ("fsdp", "ctx")),
            P(),
        ),
        check_vma=False,
    )
```

profile of v0, /device:TPU:0, one launch (start us, length us, event | category | flops | bytes accessed | tf_op | source)
XLA Modules:
  0.0 2533.0 jit_solution(4475514019620308846)
XLA Ops:
  42.5 21.9 all-gather.35.cloned.1.call-done
  92.1 19.6 fusion.297
  136.2 48.1 %reduce-scatter.31.cloned.1.call-done = bf16[256,1152]{1,0:T(8,128)(2,1)} async-done(((bf16[1024,1152]{1,0:T(8,128)(2,1)}), bf16[256,1152]{1,0:T(8,128)(2,1)}) %reduce-scatter.31.cloned.1.call-update) | async-done | bytes 589840 | tf_op jit(solution)/shard_map/reduce_scatter | solution.py:117
  187.0 50.1 %all-gather.55.cloned.1.call-done = bf16[1024,1152]{1,0:T(8,128)(2,1)} async-done(((bf16[256,1152]{1,0:T(8,128)(2,1)}), bf16[1024,1152]{1,0:T(8,128)(2,1)}) %all-gather.55.cloned.1.call-update) | async-done | bytes 2359312 | tf_op jit(solution)/shard_map/all_gather | solution.py:81
  262.6 19.5 fusion.298
  287.5 17.3 fusion.165
  309.2 48.1 %reduce-scatter.39.cloned.1.call-done = bf16[256,1152]{1,0:T(8,128)(2,1)} async-done(((bf16[1024,1152]{1,0:T(8,128)(2,1)}), bf16[256,1152]{1,0:T(8,128)(2,1)}) %reduce-scatter.39.cloned.1.call-update) | async-done | bytes 589840 | tf_op jit(solution)/shard_map/reduce_scatter | solution.py:117
  369.2 44.8 %all-gather.63.cloned.1.call-done = bf16[1024,1152]{1,0:T(8,128)(2,1)} async-done(((bf16[256,1152]{1,0:T(8,128)(2,1)}), bf16[1024,1152]{1,0:T(8,128)(2,1)}) %all-gather.63.cloned.1.call-update) | async-done | bytes 2359312 | tf_op jit(solution)/shard_map/all_gather | solution.py:81
  421.0 44.2 %all-gather.47.cloned.1.call-done = bf16[1024,1152]{1,0:T(8,128)(2,1)} async-done(((bf16[256,1152]{1,0:T(8,128)(2,1)}), bf16[1024,1152]{1,0:T(8,128)(2,1)}) %all-gather.47.cloned.1.call-update) | async-done | bytes 2359312 | tf_op jit(solution)/shard_map/all_gather | solution.py:81
  473.2 18.2 all-gather.43.cloned.1.call-done
  491.4 51.9 %all-gather.41.cloned.1.call-done = bf16[1024,1152]{1,0:T(8,128)(2,1)} async-done(((bf16[256,1152]{1,0:T(8,128)(2,1)}), bf16[1024,1152]{1,0:T(8,128)(2,1)}) %all-gather.41.cloned.1.call-update) | async-done | bytes 2359312 | tf_op jit(solution)/shard_map/all_gather | solution.py:124
  551.0 43.3 %all-gather.79.cloned.1.call-done = bf16[1,1024,1152]{2,1,0:T(8,128)(2,1)} async-done(((bf16[1,256,1152]{2,1,0:T(8,128)(2,1)}), bf16[1,1024,1152]{2,1,0:T(8,128)(2,1)}) %all-gather.79.cloned.1.call-update) | async-done | bytes 2359312 | tf_op jit(solution)/shard_map/all_gather | solution.py:125
  594.3 26.0 %all-gather.45.cloned.1.call-done = bf16[1076,1152]{0,1:T(8,128)(2,1)} async-done(((bf16[1076,288]{0,1:T(8,128)(2,1)}), bf16[1076,1152]{0,1:T(8,128)(2,1)}) %all-gather.45.cloned.1.call-update) | async-done | bytes 2479120 | tf_op jit(solution)/shard_map/all_gather | solution.py:49
  638.4 33.8 %all-gather.61.cloned.1.call-done = bf16[1024,1152]{1,0:T(8,128)(2,1)} async-done(((bf16[256,1152]{1,0:T(8,128)(2,1)}), bf16[1024,1152]{1,0:T(8,128)(2,1)}) %all-gather.61.cloned.1.call-update) | async-done | bytes 2359312 | tf_op jit(solution)/shard_map/all_gather | solution.py:124
  679.9 43.1 %all-gather.83.cloned.1.call-done = bf16[1,1024,1152]{2,1,0:T(8,128)(2,1)} async-done(((bf16[1,256,1152]{2,1,0:T(8,128)(2,1)}), bf16[1,1024,1152]{2,1,0:T(8,128)(2,1)}) %all-gather.83.cloned.1.call-update) | async-done | bytes 2359312 | tf_op jit(solution)/shard_map/all_gather | solution.py:125
  749.6 19.6 fusion.300
  801.9 19.8 fusion.299
  869.8 50.5 %reduce-scatter.63.cloned.1.call-done = bf16[256,1152]{1,0:T(8,128)(2,1)} async-done(((bf16[1024,1152]{1,0:T(8,128)(2,1)}), bf16[256,1152]{1,0:T(8,128)(2,1)}) %reduce-scatter.63.cloned.1.call-update) | async-done | bytes 589840 | tf_op jit(solution)/shard_map/reduce_scatter | solution.py:144
  920.3 49.9 %reduce-scatter.43.cloned.1.call-done = bf16[256,1152]{1,0:T(8,128)(2,1)} async-done(((bf16[1024,1152]{1,0:T(8,128)(2,1)}), bf16[256,1152]{1,0:T(8,128)(2,1)}) %reduce-scatter.43.cloned.1.call-update) | async-done | bytes 589840 | tf_op jit(solution)/shard_map/reduce_scatter | solution.py:117
  970.1 49.7 %reduce-scatter.35.cloned.1.call-done = bf16[256,1152]{1,0:T(8,128)(2,1)} async-done(((bf16[1024,1152]{1,0:T(8,128)(2,1)}), bf16[256,1152]{1,0:T(8,128)(2,1)}) %reduce-scatter.35.cloned.1.call-update) | async-done | bytes 589840 | tf_op jit(solution)/shard_map/reduce_scatter | solution.py:117
  1023.6 46.1 %reduce-scatter.41.cloned.1.call-done = bf16[256,1152]{1,0:T(8,128)(2,1)} async-done(((bf16[1024,1152]{1,0:T(8,128)(2,1)}), bf16[256,1152]{1,0:T(8,128)(2,1)}) %reduce-scatter.41.cloned.1.call-update) | async-done | bytes 589840 | tf_op jit(solution)/shard_map/reduce_scatter | solution.py:130
  1080.6 38.8 %reduce-scatter.33.cloned.1.call-done = bf16[256,1152]{1,0:T(8,128)(2,1)} async-done(((bf16[1024,1152]{1,0:T(8,128)(2,1)}), bf16[256,1152]{1,0:T(8,128)(2,1)}) %reduce-scatter.33.cloned.1.call-update) | async-done | bytes 589840 | tf_op jit(solution)/shard_map/reduce_scatter | solution.py:130
  1127.9 43.0 %all-gather.75.cloned.1.call-done = bf16[1024,1152]{1,0:T(8,128)(2,1)} async-done(((bf16[256,1152]{1,0:T(8,128)(2,1)}), bf16[1024,1152]{1,0:T(8,128)(2,1)}) %all-gather.75.cloned.1.call-update) | async-done | bytes 2359312 | tf_op jit(solution)/shard_map/all_gather | solution.py:160
  1173.6 21.9 multiply_reduce_fusion.1
  1195.5 27.9 %multiply_convert_fusion.1 = bf16[4,1024,2048]{2,1,0:T(8,128)(2,1)} fusion(f32[4,1024,2048]{2,1,0:T(8,128)} %get-tuple-element.135, f32[4,1024]{1,0:T(4,128)S(1)} %get-tuple-element.134, f32[4,1024,2048]{2,1,0:T(8,128)} %get-tuple-element.129, f32[4,1024]{1,0:T(4,128)S(1)} %copy-done.132), kind=kLoop, calls=%fused_computation.6 | loop fusion | flops 33554432 | bytes 83918848 | tf_op jit(solution)/shard_map/convert_element_type | solution.py:175
  1289.8 34.8 %all-gather.53.cloned.1.call-done = bf16[1024,1152]{1,0:T(8,128)(2,1)} async-done(((bf16[256,1152]{1,0:T(8,128)(2,1)}), bf16[1024,1152]{1,0:T(8,128)(2,1)}) %all-gather.53.cloned.1.call-update) | async-done | bytes 2359312 | tf_op jit(solution)/shard_map/all_gather | solution.py:124
  1332.2 43.2 %all-gather.81.cloned.1.call-done = bf16[1,1024,1152]{2,1,0:T(8,128)(2,1)} async-done(((bf16[1,256,1152]{2,1,0:T(8,128)(2,1)}), bf16[1,1024,1152]{2,1,0:T(8,128)(2,1)}) %all-gather.81.cloned.1.call-update) | async-done | bytes 2359312 | tf_op jit(solution)/shard_map/all_gather | solution.py:125
  1446.5 26.7 %reduce-scatter.71.cloned.1.call-done = bf16[256,1152]{1,0:T(8,128)(2,1)} async-done(((bf16[1024,1152]{1,0:T(8,128)(2,1)}), bf16[256,1152]{1,0:T(8,128)(2,1)}) %reduce-scatter.71.cloned.1.call-update) | async-done | bytes 589840 | tf_op jit(solution)/shard_map/reduce_scatter | solution.py:144
  1473.3 49.9 %reduce-scatter.55.cloned.1.call-done = bf16[256,1152]{1,0:T(8,128)(2,1)} async-done(((bf16[1024,1152]{1,0:T(8,128)(2,1)}), bf16[256,1152]{1,0:T(8,128)(2,1)}) %reduce-scatter.55.cloned.1.call-update) | async-done | bytes 589840 | tf_op jit(solution)/shard_map/reduce_scatter | solution.py:144
  1523.2 49.7 %reduce-scatter.69.cloned.1.call-done = bf16[256,1152]{1,0:T(8,128)(2,1)} async-done(((bf16[1024,1152]{1,0:T(8,128)(2,1)}), bf16[256,1152]{1,0:T(8,128)(2,1)}) %reduce-scatter.69.cloned.1.call-update) | async-done | bytes 589840 | tf_op jit(solution)/shard_map/reduce_scatter | solution.py:206
  1577.0 45.6 %reduce-scatter.37.cloned.1.call-done = bf16[256,1152]{1,0:T(8,128)(2,1)} async-done(((bf16[1024,1152]{1,0:T(8,128)(2,1)}), bf16[256,1152]{1,0:T(8,128)(2,1)}) %reduce-scatter.37.cloned.1.call-update) | async-done | bytes 589840 | tf_op jit(solution)/shard_map/reduce_scatter | solution.py:130
  1625.8 47.3 %reduce-scatter.45.cloned.1.call-done = bf16[256,1152]{1,0:T(8,128)(2,1)} async-done(((bf16[1024,1152]{1,0:T(8,128)(2,1)}), bf16[256,1152]{1,0:T(8,128)(2,1)}) %reduce-scatter.45.cloned.1.call-update) | async-done | bytes 589840 | tf_op jit(solution)/shard_map/reduce_scatter | solution.py:130
  1681.9 48.4 %all-gather.71.cloned.1.call-done = bf16[1024,1152]{1,0:T(8,128)(2,1)} async-done(((bf16[256,1152]{1,0:T(8,128)(2,1)}), bf16[1024,1152]{1,0:T(8,128)(2,1)}) %all-gather.71.cloned.1.call-update) | async-done | bytes 2359312 | tf_op jit(solution)/shard_map/all_gather | solution.py:160
  1758.6 22.5 all-gather.77.cloned.1.call-done
  1783.8 48.8 %all-gather.73.cloned.1.call-done = bf16[1024,1152]{1,0:T(8,128)(2,1)} async-done(((bf16[256,1152]{1,0:T(8,128)(2,1)}), bf16[1024,1152]{1,0:T(8,128)(2,1)}) %all-gather.73.cloned.1.call-update) | async-done | bytes 2359312 | tf_op jit(solution)/shard_map/all_gather | solution.py:160
  1869.5 22.0 multiply_reduce_fusion.3
  1891.5 28.4 %multiply_convert_fusion.3 = bf16[4,1024,2048]{2,1,0:T(8,128)(2,1)} fusion(f32[4,1024,2048]{2,1,0:T(8,128)} %get-tuple-element.137, f32[4,1024]{1,0:T(4,128)S(1)} %get-tuple-element.136, f32[4,1024,2048]{2,1,0:T(8,128)} %get-tuple-element.127, f32[4,1024]{1,0:T(4,128)S(1)} %copy-done.125), kind=kLoop, calls=%fused_computation.10 | loop fusion | flops 33554432 | bytes 83918848 | tf_op jit(solution)/shard_map/convert_element_type | solution.py:175
  1920.0 25.2 multiply_reduce_fusion.2
  1951.6 28.3 %multiply_convert_fusion.2 = bf16[4,1024,2048]{2,1,0:T(8,128)(2,1)} fusion(f32[4,1024,2048]{2,1,0:T(8,128)} %get-tuple-element.139, f32[4,1024]{1,0:T(4,128)S(1)} %get-tuple-element.138, f32[4,1024,2048]{2,1,0:T(8,128)} %get-tuple-element.131, f32[4,1024]{1,0:T(4,128)S(1)} %copy-done.130), kind=kLoop, calls=%fused_computation.8 | loop fusion | flops 33554432 | bytes 83918848 | tf_op jit(solution)/shard_map/convert_element_type | solution.py:175
  1979.9 25.2 multiply_reduce_fusion
  2011.4 28.3 %multiply_convert_fusion = bf16[4,1024,2048]{2,1,0:T(8,128)(2,1)} fusion(f32[4,1024,2048]{2,1,0:T(8,128)} %get-tuple-element.141, f32[4,1024]{1,0:T(4,128)S(1)} %get-tuple-element.140, f32[4,1024,2048]{2,1,0:T(8,128)} %get-tuple-element.133, f32[4,1024]{1,0:T(4,128)S(1)} %copy-done.128), kind=kLoop, calls=%fused_computation.4 | loop fusion | flops 33554432 | bytes 83918848 | tf_op jit(solution)/shard_map/convert_element_type | solution.py:175
  2210.2 31.2 %reduce-scatter.79.cloned.1.call-done = bf16[144,288]{1,0:T(8,128)(2,1)} async-done(((bf16[1152,288]{1,0:T(8,128)(2,1)}), bf16[144,288]{1,0:T(8,128)(2,1)}) %reduce-scatter.79.cloned.1.call-update) | async-done | bytes 82960 | tf_op jit(solution)/shard_map/reduce_scatter | solution.py:218
  2247.5 32.2 %reduce-scatter.83.cloned.1.call-done = bf16[144,288]{1,0:T(8,128)(2,1)} async-done(((bf16[1152,288]{1,0:T(8,128)(2,1)}), bf16[144,288]{1,0:T(8,128)(2,1)}) %reduce-scatter.83.cloned.1.call-update) | async-done | bytes 82960 | tf_op jit(solution)/shard_map/reduce_scatter | solution.py:224
  2281.3 36.9 %reduce-scatter.81.cloned.1.call-done = bf16[144,288]{1,0:T(8,128)(2,1)} async-done(((bf16[1152,288]{1,0:T(8,128)(2,1)}), bf16[144,288]{1,0:T(8,128)(2,1)}) %reduce-scatter.81.cloned.1.call-update) | async-done | bytes 82960 | tf_op jit(solution)/shard_map/reduce_scatter | solution.py:221
  2319.8 48.8 %reduce-scatter.53.cloned.1.call-done = bf16[256,1152]{1,0:T(8,128)(2,1)} async-done(((bf16[1024,1152]{1,0:T(8,128)(2,1)}), bf16[256,1152]{1,0:T(8,128)(2,1)}) %reduce-scatter.53.cloned.1.call-update) | async-done | bytes 589840 | tf_op jit(solution)/shard_map/reduce_scatter | solution.py:206
  2368.6 49.9 %reduce-scatter.61.cloned.1.call-done = bf16[256,1152]{1,0:T(8,128)(2,1)} async-done(((bf16[1024,1152]{1,0:T(8,128)(2,1)}), bf16[256,1152]{1,0:T(8,128)(2,1)}) %reduce-scatter.61.cloned.1.call-update) | async-done | bytes 589840 | tf_op jit(solution)/shard_map/reduce_scatter | solution.py:206
  2418.5 49.9 %reduce-scatter.77.cloned.1.call-done = bf16[256,1152]{1,0:T(8,128)(2,1)} async-done(((bf16[1024,1152]{1,0:T(8,128)(2,1)}), bf16[256,1152]{1,0:T(8,128)(2,1)}) %reduce-scatter.77.cloned.1.call-update) | async-done | bytes 589840 | tf_op jit(solution)/shard_map/reduce_scatter | solution.py:206
  2483.4 42.4 %all-reduce = (f32[1152]{0:T(1024)}, f32[1152]{0:T(1024)}, f32[1152]{0:T(1024)}, f32[1152]{0:T(1024)}, f32[1152]{0:T(1024)}, /*index=5*/f32[1152]{0:T(1024)}, f32[1152]{0:T(1024)}, f32[4304]{0:T(1024)}, f32[1152]{0:T(1024)}) all-reduce(f32[1152]{0:T(1024)S(1)} %copy-done.115, ...), channel_id=1, replica_groups=mesh['fsdp'=4,'ctx'=2,'tp'=4] {'fsdp','ctx','tp'}, use_global_device_ids=true, to_apply=%region_72.73 | all-reduce | flops 13520 | bytes 108160 | tf_op jit(solution)/shard_map/psum | solution.py:240
  (763 shorter events, 752.5 us)
Async XLA Ops:
  251.4 105.9 %reduce-scatter.39.cloned.1.call-start = ((), (), s32[]{:S(2)}) async-start(), calls=%async_computation.47 | async-start | bytes 2949120 | tf_op jit(solution)/shard_map/reduce_scatter | solution.py:117
  309.1 104.9 %all-gather.63.cloned.1.call-start = ((), (), s32[]{:S(2)}) async-start(), calls=%async_computation.50 | async-start | bytes 2949120 | tf_op jit(solution)/shard_map/all_gather | solution.py:81
  363.8 101.5 %all-gather.47.cloned.1.call-start = ((), (), s32[]{:S(2)}) async-start(), calls=%async_computation.38 | async-start | bytes 2949120 | tf_op jit(solution)/shard_map/all_gather | solution.py:81
  364.4 127.0 %all-gather.43.cloned.1.call-start = ((), (), s32[]{:S(2)}) async-start(), calls=%async_computation.35 | async-start | bytes 3317760 | tf_op jit(solution)/shard_map/all_gather | solution.py:48
  365.1 178.3 %all-gather.41.cloned.1.call-start = ((), (), s32[]{:S(2)}) async-start(), calls=%async_computation.34 | async-start | bytes 2949120 | tf_op jit(solution)/shard_map/all_gather | solution.py:124
  365.7 228.6 %all-gather.79.cloned.1.call-start = ((), (), s32[]{:S(2)}) async-start(), calls=%async_computation.82 | async-start | bytes 2949120 | tf_op jit(solution)/shard_map/all_gather | solution.py:125
  367.2 253.1 %all-gather.45.cloned.1.call-start = ((), (), s32[]{:S(2)}) async-start(), calls=%async_computation.36 | async-start | bytes 3317760 | tf_op jit(solution)/shard_map/all_gather | solution.py:49
  367.8 304.4 %all-gather.61.cloned.1.call-start = ((), (), s32[]{:S(2)}) async-start(), calls=%async_computation.48 | async-start | bytes 2949120 | tf_op jit(solution)/shard_map/all_gather | solution.py:124
  368.4 354.6 %all-gather.83.cloned.1.call-start = ((), (), s32[]{:S(2)}) async-start(), calls=%async_computation.84 | async-start | bytes 2949120 | tf_op jit(solution)/shard_map/all_gather | solution.py:125
  369.0 380.6 %all-gather.67.cloned.1.call-start = ((), (), s32[]{:S(2)}) async-start(), calls=%async_computation.52 | async-start | bytes 1769472 | tf_op jit(solution)/shard_map/all_gather | solution.py:87
  417.5 352.8 %all-gather.65.cloned.1.call-start = ((), (), s32[]{:S(2)}) async-start(), calls=%async_computation.51 | async-start | bytes 1769472 | tf_op jit(solution)/shard_map/all_gather | solution.py:88
  421.0 380.9 %all-gather.51.cloned.1.call-start = ((), (), s32[]{:S(2)}) async-start(), calls=%async_computation.40 | async-start | bytes 1769472 | tf_op jit(solution)/shard_map/all_gather | solution.py:87
  468.8 352.9 %all-gather.49.cloned.1.call-start = ((), (), s32[]{:S(2)}) async-start(), calls=%async_computation.39 | async-start | bytes 1769472 | tf_op jit(solution)/shard_map/all_gather | solution.py:88
  473.1 396.7 %reduce-scatter.47.cloned.1.call-start = ((), (), s32[]{:S(2)}) async-start(), calls=%async_computation.56 | async-start | bytes 2949120 | tf_op jit(solution)/shard_map/reduce_scatter | solution.py:144
  638.1 282.1 %reduce-scatter.63.cloned.1.call-start = ((), (), s32[]{:S(2)}) async-start(), calls=%async_computation.66 | async-start | bytes 2949120 | tf_op jit(solution)/shard_map/reduce_scatter | solution.py:144
  739.2 231.0 %reduce-scatter.43.cloned.1.call-start = ((), (), s32[]{:S(2)}) async-start(), calls=%async_computation.53 | async-start | bytes 2949120 | tf_op jit(solution)/shard_map/reduce_scatter | solution.py:117
  791.5 228.4 %reduce-scatter.35.cloned.1.call-start = ((), (), s32[]{:S(2)}) async-start(), calls=%async_computation.41 | async-start | bytes 2949120 | tf_op jit(solution)/shard_map/reduce_scatter | solution.py:117
  840.9 228.9 %reduce-scatter.41.cloned.1.call-start = ((), (), s32[]{:S(2)}) async-start(), calls=%async_computation.49 | async-start | bytes 2949120 | tf_op jit(solution)/shard_map/reduce_scatter | solution.py:130
  850.0 269.5 %reduce-scatter.33.cloned.1.call-start = ((), (), s32[]{:S(2)}) async-start(), calls=%async_computation.37 | async-start | bytes 2949120 | tf_op jit(solution)/shard_map/reduce_scatter | solution.py:130
  859.0 311.9 %all-gather.75.cloned.1.call-start = ((), (), s32[]{:S(2)}) async-start(), calls=%async_computation.67 | async-start | bytes 2949120 | tf_op jit(solution)/shard_map/all_gather | solution.py:160
  1076.3 173.8 %all-gather.69.cloned.1.call-start = ((), (), s32[]{:S(2)}) async-start(), calls=%async_computation.54 | async-start | bytes 2949120 | tf_op jit(solution)/shard_map/all_gather | solution.py:124
  1125.7 147.5 %all-gather.85.cloned.1.call-start = ((), (), s32[]{:S(2)}) async-start(), calls=%async_computation.85 | async-start | bytes 2949120 | tf_op jit(solution)/shard_map/all_gather | solution.py:125
  1126.5 198.1 %all-gather.53.cloned.1.call-start = ((), (), s32[]{:S(2)}) async-start(), calls=%async_computation.42 | async-start | bytes 2949120 | tf_op jit(solution)/shard_map/all_gather | solution.py:124
  1127.1 248.4 %all-gather.81.cloned.1.call-start = ((), (), s32[]{:S(2)}) async-start(), calls=%async_computation.83 | async-start | bytes 2949120 | tf_op jit(solution)/shard_map/all_gather | solution.py:125
  1127.8 279.8 %reduce-scatter.65.cloned.1.call-start = ((), (), s32[]{:S(2)}) async-start(), calls=%async_computation.68 | async-start | bytes 1769472 | tf_op jit(solution)/shard_map/reduce_scatter | solution.py:189
  1233.3 189.0 %reduce-scatter.67.cloned.1.call-start = ((), (), s32[]{:S(2)}) async-start(), calls=%async_computation.69 | async-start | bytes 1769472 | tf_op jit(solution)/shard_map/reduce_scatter | solution.py:192
  1249.9 223.4 %reduce-scatter.71.cloned.1.call-start = ((), (), s32[]{:S(2)}) async-start(), calls=%async_computation.71 | async-start | bytes 2949120 | tf_op jit(solution)/shard_map/reduce_scatter | solution.py:144
  1289.5 233.7 %reduce-scatter.55.cloned.1.call-start = ((), (), s32[]{:S(2)}) async-start(), calls=%async_computation.61 | async-start | bytes 2949120 | tf_op jit(solution)/shard_map/reduce_scatter | solution.py:144
  1391.7 181.2 %reduce-scatter.69.cloned.1.call-start = ((), (), s32[]{:S(2)}) async-start(), calls=%async_computation.70 | async-start | bytes 2949120 | tf_op jit(solution)/shard_map/reduce_scatter | solution.py:206
  1427.9 194.7 %reduce-scatter.37.cloned.1.call-start = ((), (), s32[]{:S(2)}) async-start(), calls=%async_computation.43 | async-start | bytes 2949120 | tf_op jit(solution)/shard_map/reduce_scatter | solution.py:130
  1436.1 236.9 %reduce-scatter.45.cloned.1.call-start = ((), (), s32[]{:S(2)}) async-start(), calls=%async_computation.55 | async-start | bytes 2949120 | tf_op jit(solution)/shard_map/reduce_scatter | solution.py:130
  1445.1 285.1 %all-gather.71.cloned.1.call-start = ((), (), s32[]{:S(2)}) async-start(), calls=%async_computation.57 | async-start | bytes 2949120 | tf_op jit(solution)/shard_map/all_gather | solution.py:160
  1680.8 151.8 %all-gather.73.cloned.1.call-start = ((), (), s32[]{:S(2)}) async-start(), calls=%async_computation.62 | async-start | bytes 2949120 | tf_op jit(solution)/shard_map/all_gather | solution.py:160
  1681.6 462.2 %reduce-scatter.51.cloned.1.call-start = ((), (), s32[]{:S(2)}) async-start(), calls=%async_computation.59 | async-start | bytes 1769472 | tf_op jit(solution)/shard_map/reduce_scatter | solution.py:192
  1749.5 398.7 %reduce-scatter.59.cloned.1.call-start = ((), (), s32[]{:S(2)}) async-start(), calls=%async_computation.64 | async-start | bytes 1769472 | tf_op jit(solution)/shard_map/reduce_scatter | solution.py:192
  1869.4 285.6 %reduce-scatter.75.cloned.1.call-start = ((), (), s32[]{:S(2)}) async-start(), calls=%async_computation.74 | async-start | bytes 1769472 | tf_op jit(solution)/shard_map/reduce_scatter | solution.py:192
  1891.5 268.3 %reduce-scatter.49.cloned.1.call-start = ((), (), s32[]{:S(2)}) async-start(), calls=%async_computation.58 | async-start | bytes 1769472 | tf_op jit(solution)/shard_map/reduce_scatter | solution.py:189
  1951.5 212.7 %reduce-scatter.57.cloned.1.call-start = ((), (), s32[]{:S(2)}) async-start(), calls=%async_computation.63 | async-start | bytes 1769472 | tf_op jit(solution)/shard_map/reduce_scatter | solution.py:189
  2011.4 159.6 %reduce-scatter.73.cloned.1.call-start = ((), (), s32[]{:S(2)}) async-start(), calls=%async_computation.73 | async-start | bytes 1769472 | tf_op jit(solution)/shard_map/reduce_scatter | solution.py:189
  2049.6 150.4 %reduce-scatter.89.cloned.1.call-start = ((), (), s32[]{:S(2)}) async-start(), calls=%async_computation.81 | async-start | bytes 2985984 | tf_op jit(solution)/shard_map/reduce_scatter | solution.py:233
  2069.4 132.4 %reduce-scatter.87.cloned.1.call-start = ((), (), s32[]{:S(2)}) async-start(), calls=%async_computation.80 | async-start | bytes 2985984 | tf_op jit(solution)/shard_map/reduce_scatter | solution.py:230
  2088.1 120.3 %reduce-scatter.85.cloned.1.call-start = ((), (), s32[]{:S(2)}) async-start(), calls=%async_computation.79 | async-start | bytes 995328 | tf_op jit(solution)/shard_map/reduce_scatter | solution.py:227
  2134.2 107.1 %reduce-scatter.79.cloned.1.call-start = ((), (), s32[]{:S(2)}) async-start(), calls=%async_computation.76 | async-start | bytes 995328 | tf_op jit(solution)/shard_map/reduce_scatter | solution.py:218
  2143.5 136.2 %reduce-scatter.83.cloned.1.call-start = ((), (), s32[]{:S(2)}) async-start(), calls=%async_computation.78 | async-start | bytes 995328 | tf_op jit(solution)/shard_map/reduce_scatter | solution.py:224
  2159.7 158.5 %reduce-scatter.81.cloned.1.call-start = ((), (), s32[]{:S(2)}) async-start(), calls=%async_computation.77 | async-start | bytes 995328 | tf_op jit(solution)/shard_map/reduce_scatter | solution.py:221
  2175.8 192.8 %reduce-scatter.53.cloned.1.call-start = ((), (), s32[]{:S(2)}) async-start(), calls=%async_computation.60 | async-start | bytes 2949120 | tf_op jit(solution)/shard_map/reduce_scatter | solution.py:206
  2182.3 236.1 %reduce-scatter.61.cloned.1.call-start = ((), (), s32[]{:S(2)}) async-start(), calls=%async_computation.65 | async-start | bytes 2949120 | tf_op jit(solution)/shard_map/reduce_scatter | solution.py:206
  2189.7 278.6 %reduce-scatter.77.cloned.1.call-start = ((), (), s32[]{:S(2)}) async-start(), calls=%async_computation.75 | async-start | bytes 2949120 | tf_op jit(solution)/shard_map/reduce_scatter | solution.py:206
  (230 other events, 7030.5 us)
Sparse Core Ops, SparseCore 0:
  11.2 53.1 all-gather.34
  92.0 22.7 all-gather.36
  136.3 48.0 reduce-scatter.30
  187.1 49.9 all-gather.54
  264.7 22.7 all-gather.56
  309.2 48.0 reduce-scatter.38
  363.9 49.9 all-gather.62
  416.0 49.2 all-gather.46
  466.8 24.5 all-gather.42
  492.9 50.4 all-gather.40
  544.9 49.2 all-gather.78
  595.7 24.5 all-gather.44
  621.7 50.4 all-gather.60
  673.6 49.2 all-gather.82
  724.4 21.6 all-gather.66
  747.5 22.7 all-gather.64
  771.8 22.7 all-gather.50
  796.0 22.7 all-gather.48
  821.7 48.0 reduce-scatter.46
  872.7 47.5 reduce-scatter.62
  922.6 47.5 reduce-scatter.42
  972.3 47.5 reduce-scatter.34
  1022.2 47.5 reduce-scatter.40
  1071.9 47.5 reduce-scatter.32
  1120.9 49.9 all-gather.74
  1173.0 49.2 all-gather.68
  1223.9 49.2 all-gather.84
  1275.2 49.2 all-gather.52
  1326.2 49.2 all-gather.80
  1400.5 21.7 reduce-scatter.66
  1425.2 48.0 reduce-scatter.70
  1475.6 47.5 reduce-scatter.54
  1525.3 47.5 reduce-scatter.68
  1575.0 47.5 reduce-scatter.36
  1625.5 47.5 reduce-scatter.44
  1680.2 49.9 all-gather.70
  1731.8 49.2 all-gather.76
  1783.3 49.2 all-gather.72
  1892.4 21.7 reduce-scatter.74
  2072.5 43.7 reduce-scatter.88
  2120.6 43.7 reduce-scatter.86
  2167.6 35.0 reduce-scatter.84
  2206.2 35.0 reduce-scatter.78
  2244.6 35.0 reduce-scatter.82
  2283.1 35.0 reduce-scatter.80
  2320.5 48.0 reduce-scatter.52
  2370.9 47.5 reduce-scatter.60
  2420.8 47.5 reduce-scatter.76
  (8 shorter events, 163.2 us)
where the time goes:
time: 2540 us; the launch traced here: 2530 us
  waiting for transfers between devices  1480 us (58%)
  matrix products  703 us (28%)
  other arithmetic  204 us (8%)
  blocking collectives  100 us (4%)
    dot_general x72, matrix products, matmul(): return jnp.dot(left, right, preferred_element_type=jnp.float32)  320 us
    reduce_scatter x4, waiting for transfers between devices, shards(): lax.psum_scatter(normed_term.astype(jnp.bfloat16), 'tp', scatter_dimensio...  198 us
    reduce_scatter x4, waiting for transfers between devices, shards(): lax.psum_scatter(matmul(attended, wo_all).astype(jnp.bfloat16), 'tp', sca...  196 us
    reduce_scatter x4, waiting for transfers between devices, shards(): lax.psum_scatter(matmul(active, second_use).astype(jnp.bfloat16), 'tp', s...  178 us
    all_gather x4, waiting for transfers between devices, shards(): d_attention_all = lax.all_gather(d_attention, 'tp', axis=0, tiled=True)  163 us
    all_gather x4, waiting for transfers between devices, shards(): normed_all = lax.all_gather(normed, 'tp', axis=0, tiled=True)  161 us
    all_gather x4, waiting for transfers between devices, shards(): lax.all_gather(row_cot, 'tp', axis=0, tiled=True)  145 us
    reduce_scatter x4, waiting for transfers between devices, shards(): lax.psum_scatter(matmul(d_before, first_use.T).astype(jnp.bfloat16), 'tp'...  138 us
  transfers between devices with their start and end apart: 56, of which 41 were waited for; matrix products, arithmetic and copies ran while one was open for 33% of the time, Pallas kernels for 0%

commit v1 on v0

--- a/solution.py
+++ b/solution.py
@@ -7,6 +7,19 @@
 HD = 72
 FF = 4304
 EPSILON = 1e-06
+
+
+def gather_around(array, axis, dim):
+    ways = lax.axis_size(axis)
+    up = [(d, (d + 1) % ways) for d in range(ways)]
+    down = [(d, (d - 1) % ways) for d in range(ways)]
+    earlier, later = ([array], [array])
+    for _ in range(ways // 2):
+        earlier.append(lax.ppermute(earlier[-1], axis, up))
+    for _ in range((ways - 1) // 2):
+        later.append(lax.ppermute(later[-1], axis, down))
+    line = jnp.concatenate([*earlier[::-1], *later[1:]], axis=dim)
+    return jnp.roll(line, (lax.axis_index(axis) - ways // 2) * array.shape[dim], axis=dim)
 
 
 def layer_norm(values, gain, bias):
@@ -121,7 +134,7 @@
         )
         normed_two = layer_norm(hidden, ln2_gain, ln2_bias).astype(jnp.bfloat16)
         normed_two_all, cot_all = (
-            lax.all_gather(normed_two, "tp", axis=0, tiled=True),
+            gather_around(normed_two, "tp", 0),
             lax.all_gather(row_cot, "tp", axis=0, tiled=True),
         )
         before = matmul(normed_two_all, first_use) + first_bias

time: 2540 us -> 2450 us (0.965)
  waiting for transfers between devices: 1480 us -> 1310 us
  other arithmetic: 204 us -> 249 us
  starting transfers between devices: 7.18 us -> 43.6 us
    ppermute x0 -> x12, waiting for transfers between devices: none -> 168 us  [the longest x4 138 us: gather_around(): later.append(lax.ppermute(later[-1], axis, down))]
    all_gather x4 -> x0, waiting for transfers between devices: 121 us -> none  [shards(): lax.all_gather(normed_two, 'tp', axis=0, tiled=True)]
    all_gather x4, waiting for transfers between devices: 145 us -> 42.3 us  [shards(): lax.all_gather(row_cot, 'tp', axis=0, tiled=True)]
    reduce_scatter x4, waiting for transfers between devices: 138 us -> 45.5 us  [shards(): lax.psum_scatter(matmul(d_before, first_use.T).astype(jnp.bfloat16), 'tp'...]
    concatenate x0 -> x4, other arithmetic: none -> 44.6 us  [gather_around(): jnp.roll(line, (lax.axis_index(axis) - ways // 2) * array.shape[dim], axi...]
    ppermute x0 -> x12, starting transfers between devices: none -> 37.2 us  [the longest x8 29.9 us: gather_around(): earlier.append(lax.ppermute(earlier[-1], axis, up))]
  transfers between devices with their start and end apart: 56 -> 64, of which waited for: 41 -> 35; matrix products, arithmetic and copies ran while one was open for 33% -> 36% of each run, Pallas kernels for 0% -> 0%
where the time goes in v1:
time: 2450 us; the launch traced here: 2440 us
  waiting for transfers between devices  1310 us (53%)
  matrix products  696 us (28%)
  other arithmetic  249 us (10%)
  blocking collectives  100 us (4%)
  starting transfers between devices  43.6 us (2%)
  local copies, waits for them, and re-layouts  27.9 us (1%)
    dot_general x72, matrix products, matmul(): return jnp.dot(left, right, preferred_element_type=jnp.float32)  312 us
    reduce_scatter x4, waiting for transfers between devices, shards(): lax.psum_scatter(normed_term.astype(jnp.bfloat16), 'tp', scatter_dimensio...  198 us
    reduce_scatter x4, waiting for transfers between devices, shards(): lax.psum_scatter(matmul(attended, wo_all).astype(jnp.bfloat16), 'tp', sca...  196 us
    reduce_scatter x4, waiting for transfers between devices, shards(): lax.psum_scatter(matmul(active, second_use).astype(jnp.bfloat16), 'tp', s...  177 us
    all_gather x4, waiting for transfers between devices, shards(): d_attention_all = lax.all_gather(d_attention, 'tp', axis=0, tiled=True)  175 us
    all_gather x4, waiting for transfers between devices, shards(): normed_all = lax.all_gather(normed, 'tp', axis=0, tiled=True)  140 us
    ppermute x4, waiting for transfers between devices, gather_around(): later.append(lax.ppermute(later[-1], axis, down))  138 us
    convert_element_type x4, other arithmetic, shards(): d_scores = (probs * (d_probs - weighted)).astype(jnp.bfloat16)  113 us
  transfers between devices with their start and end apart: 64, of which 35 were waited for; matrix products, arithmetic and copies ran while one was open for 36% of the time, Pallas kernels for 0%

profile of v1, /device:TPU:0, one launch (start us, length us, event | category | flops | bytes accessed | tf_op | source)
XLA Modules:
  0.0 2439.8 jit_solution(9120816702568446382)
XLA Ops:
  42.5 21.9 all-gather.31.cloned.1.call-done
  92.1 19.6 fusion.325
  114.8 17.0 fusion.187
  136.2 48.1 %reduce-scatter.31.cloned.1.call-done = bf16[256,1152]{1,0:T(8,128)(2,1)} async-done(((bf16[1024,1152]{1,0:T(8,128)(2,1)}), bf16[256,1152]{1,0:T(8,128)(2,1)}) %reduce-scatter.31.cloned.1.call-update) | async-done | bytes 589840 | tf_op jit(solution)/shard_map/reduce_scatter | solution.py:130
  187.0 50.1 %all-gather.47.cloned.1.call-done = bf16[1024,1152]{1,0:T(8,128)(2,1)} async-done(((bf16[256,1152]{1,0:T(8,128)(2,1)}), bf16[1024,1152]{1,0:T(8,128)(2,1)}) %all-gather.47.cloned.1.call-update) | async-done | bytes 2359312 | tf_op jit(solution)/shard_map/all_gather | solution.py:94
  262.6 19.5 fusion.326
  287.5 17.3 fusion.193
  309.2 48.1 %reduce-scatter.39.cloned.1.call-done = bf16[256,1152]{1,0:T(8,128)(2,1)} async-done(((bf16[1024,1152]{1,0:T(8,128)(2,1)}), bf16[256,1152]{1,0:T(8,128)(2,1)}) %reduce-scatter.39.cloned.1.call-update) | async-done | bytes 589840 | tf_op jit(solution)/shard_map/reduce_scatter | solution.py:130
  369.9 44.1 %all-gather.53.cloned.1.call-done = bf16[1024,1152]{1,0:T(8,128)(2,1)} async-done(((bf16[256,1152]{1,0:T(8,128)(2,1)}), bf16[1024,1152]{1,0:T(8,128)(2,1)}) %all-gather.53.cloned.1.call-update) | async-done | bytes 2359312 | tf_op jit(solution)/shard_map/all_gather | solution.py:94
  425.1 26.8 %collective-permute-done = bf16[256,1152]{1,0:T(8,128)(2,1)} collective-permute-done((bf16[256,1152]{1,0:T(8,128)(2,1)}, bf16[256,1152]{1,0:T(8,128)(2,1)}, u32[]{:S(2)}, u32[]{:S(2)}) %collective-permute-start) | collective-permute-done | bytes 589856 | tf_op jit(solution)/shard_map/ppermute | solution.py:18
  451.9 21.6 collective-permute-start.1
  477.4 24.2 all-gather.41.cloned.1.call-done
  538.5 42.3 %all-gather.67.cloned.1.call-done = bf16[1,1024,1152]{2,1,0:T(8,128)(2,1)} async-done(((bf16[1,256,1152]{2,1,0:T(8,128)(2,1)}), bf16[1,1024,1152]{2,1,0:T(8,128)(2,1)}) %all-gather.67.cloned.1.call-update) | async-done | bytes 2359312 | tf_op jit(solution)/shard_map/all_gather | solution.py:138
  580.8 26.1 %all-gather.39.cloned.1.call-done = bf16[1076,1152]{0,1:T(8,128)(2,1)} async-done(((bf16[1076,288]{0,1:T(8,128)(2,1)}), bf16[1076,1152]{0,1:T(8,128)(2,1)}) %all-gather.39.cloned.1.call-update) | async-done | bytes 2479120 | tf_op jit(solution)/shard_map/all_gather | solution.py:62
  626.9 49.6 %collective-permute-done.8 = bf16[256,1152]{1,0:T(8,128)(2,1)S(1)} collective-permute-done((bf16[256,1152]{1,0:T(8,128)(2,1)S(1)}, bf16[256,1152]{1,0:T(8,128)(2,1)S(1)}, u32[]{:S(2)}, u32[]{:S(2)}) %collective-permute-start.8) | collective-permute-done | bytes 589856 | tf_op jit(solution)/shard_map/ppermute | solution.py:20
  726.8 19.6 fusion.328
  746.4 16.9 fusion.196
  778.0 19.6 fusion.327
  835.3 45.5 %reduce-scatter.63.cloned.1.call-done = bf16[256,1152]{1,0:T(8,128)(2,1)} async-done(((bf16[1024,1152]{1,0:T(8,128)(2,1)}), bf16[256,1152]{1,0:T(8,128)(2,1)}) %reduce-scatter.63.cloned.1.call-update) | async-done | bytes 589840 | tf_op jit(solution)/shard_map/reduce_scatter | solution.py:157
  880.8 49.9 %reduce-scatter.43.cloned.1.call-done = bf16[256,1152]{1,0:T(8,128)(2,1)} async-done(((bf16[1024,1152]{1,0:T(8,128)(2,1)}), bf16[256,1152]{1,0:T(8,128)(2,1)}) %reduce-scatter.43.cloned.1.call-update) | async-done | bytes 589840 | tf_op jit(solution)/shard_map/reduce_scatter | solution.py:130
  930.7 49.9 %reduce-scatter.35.cloned.1.call-done = bf16[256,1152]{1,0:T(8,128)(2,1)} async-done(((bf16[1024,1152]{1,0:T(8,128)(2,1)}), bf16[256,1152]{1,0:T(8,128)(2,1)}) %reduce-scatter.35.cloned.1.call-update) | async-done | bytes 589840 | tf_op jit(solution)/shard_map/reduce_scatter | solution.py:130
  984.3 46.2 %reduce-scatter.41.cloned.1.call-done = bf16[256,1152]{1,0:T(8,128)(2,1)} async-done(((bf16[1024,1152]{1,0:T(8,128)(2,1)}), bf16[256,1152]{1,0:T(8,128)(2,1)}) %reduce-scatter.41.cloned.1.call-update) | async-done | bytes 589840 | tf_op jit(solution)/shard_map/reduce_scatter | solution.py:143
  1042.2 38.0 %reduce-scatter.33.cloned.1.call-done = bf16[256,1152]{1,0:T(8,128)(2,1)} async-done(((bf16[1024,1152]{1,0:T(8,128)(2,1)}), bf16[256,1152]{1,0:T(8,128)(2,1)}) %reduce-scatter.33.cloned.1.call-update) | async-done | bytes 589840 | tf_op jit(solution)/shard_map/reduce_scatter | solution.py:143
  1086.9 55.2 %all-gather.63.cloned.1.call-done = bf16[1024,1152]{1,0:T(8,128)(2,1)} async-done(((bf16[256,1152]{1,0:T(8,128)(2,1)}), bf16[1024,1152]{1,0:T(8,128)(2,1)}) %all-gather.63.cloned.1.call-update) | async-done | bytes 2359312 | tf_op jit(solution)/shard_map/all_gather | solution.py:173
  1144.9 22.3 multiply_reduce_fusion.1
  1167.2 27.9 %multiply_convert_fusion.1 = bf16[4,1024,2048]{2,1,0:T(8,128)(2,1)} fusion(f32[4,1024,2048]{2,1,0:T(8,128)} %get-tuple-element.136, f32[4,1024]{1,0:T(4,128)S(1)} %get-tuple-element.135, f32[4,1024,2048]{2,1,0:T(8,128)} %get-tuple-element.130, f32[4,1024]{1,0:T(4,128)S(1)} %copy-done.135), kind=kLoop, calls=%fused_computation.6 | loop fusion | flops 33554432 | bytes 83918848 | tf_op jit(solution)/shard_map/convert_element_type | solution.py:188
  1207.8 54.0 %collective-permute-done.11 = bf16[256,1152]{1,0:T(8,128)(2,1)S(1)} collective-permute-done((bf16[256,1152]{1,0:T(8,128)(2,1)}, bf16[256,1152]{1,0:T(8,128)(2,1)S(1)}, u32[]{:S(2)}, u32[]{:S(2)}) %collective-permute-start.11) | collective-permute-done | bytes 589856 | tf_op jit(solution)/shard_map/ppermute | solution.py:20
  1316.3 34.9 %collective-permute-done.5 = bf16[256,1152]{1,0:T(8,128)(2,1)S(1)} collective-permute-done((bf16[256,1152]{1,0:T(8,128)(2,1)S(1)}, bf16[256,1152]{1,0:T(8,128)(2,1)S(1)}, u32[]{:S(2)}, u32[]{:S(2)}) %collective-permute-start.5) | collective-permute-done | bytes 589856 | tf_op jit(solution)/shard_map/ppermute | solution.py:20
  1430.9 49.6 %reduce-scatter.69.cloned.1.call-done = bf16[256,1152]{1,0:T(8,128)(2,1)} async-done(((bf16[1024,1152]{1,0:T(8,128)(2,1)}), bf16[256,1152]{1,0:T(8,128)(2,1)}) %reduce-scatter.69.cloned.1.call-update) | async-done | bytes 589840 | tf_op jit(solution)/shard_map/reduce_scatter | solution.py:219
  1484.6 45.6 %reduce-scatter.37.cloned.1.call-done = bf16[256,1152]{1,0:T(8,128)(2,1)} async-done(((bf16[1024,1152]{1,0:T(8,128)(2,1)}), bf16[256,1152]{1,0:T(8,128)(2,1)}) %reduce-scatter.37.cloned.1.call-update) | async-done | bytes 589840 | tf_op jit(solution)/shard_map/reduce_scatter | solution.py:143
  1533.4 47.2 %reduce-scatter.45.cloned.1.call-done = bf16[256,1152]{1,0:T(8,128)(2,1)} async-done(((bf16[1024,1152]{1,0:T(8,128)(2,1)}), bf16[256,1152]{1,0:T(8,128)(2,1)}) %reduce-scatter.45.cloned.1.call-update) | async-done | bytes 589840 | tf_op jit(solution)/shard_map/reduce_scatter | solution.py:143
  1589.1 48.7 %all-gather.59.cloned.1.call-done = bf16[1024,1152]{1,0:T(8,128)(2,1)} async-done(((bf16[256,1152]{1,0:T(8,128)(2,1)}), bf16[1024,1152]{1,0:T(8,128)(2,1)}) %all-gather.59.cloned.1.call-update) | async-done | bytes 2359312 | tf_op jit(solution)/shard_map/all_gather | solution.py:173
  1666.1 22.4 all-gather.65.cloned.1.call-done
  1691.2 48.6 %all-gather.61.cloned.1.call-done = bf16[1024,1152]{1,0:T(8,128)(2,1)} async-done(((bf16[256,1152]{1,0:T(8,128)(2,1)}), bf16[1024,1152]{1,0:T(8,128)(2,1)}) %all-gather.61.cloned.1.call-update) | async-done | bytes 2359312 | tf_op jit(solution)/shard_map/all_gather | solution.py:173
  1759.8 17.0 fusion.89
  1776.9 22.0 multiply_reduce_fusion.3
  1799.0 28.4 %multiply_convert_fusion.3 = bf16[4,1024,2048]{2,1,0:T(8,128)(2,1)} fusion(f32[4,1024,2048]{2,1,0:T(8,128)} %get-tuple-element.138, f32[4,1024]{1,0:T(4,128)S(1)} %get-tuple-element.137, f32[4,1024,2048]{2,1,0:T(8,128)} %get-tuple-element.128, f32[4,1024]{1,0:T(4,128)S(1)} %copy-done.130), kind=kLoop, calls=%fused_computation.10 | loop fusion | flops 33554432 | bytes 83918848 | tf_op jit(solution)/shard_map/convert_element_type | solution.py:188
  1827.4 25.2 %multiply_reduce_fusion.2 = (f32[4,1024]{1,0:T(4,128)S(1)}, f32[4,1024,2048]{2,1,0:T(8,128)}) fusion(f32[4,1024,2048]{2,1,0:T(8,128)} %get-tuple-element.132, f32[4,1024]{1,0:T(4,128)S(1)} %copy-done.137, bf16[1024,4,72]{0,2,1:T(8,128)(2,1)S(1)} %bitcast.667, bf16[2048,4,72]{0,2,1:T(8,128)(2,1)} %bitcast.649), kind=kOutput, calls=%fused_computation.9 | convolution fusion | flops 1233121280 | bytes 68911104 | tf_op jit(solution)/shard_map/qhd,khd->hqk/dot_general | solution.py:184
  1859.0 28.3 %multiply_convert_fusion.2 = bf16[4,1024,2048]{2,1,0:T(8,128)(2,1)} fusion(f32[4,1024,2048]{2,1,0:T(8,128)} %get-tuple-element.140, f32[4,1024]{1,0:T(4,128)S(1)} %get-tuple-element.139, f32[4,1024,2048]{2,1,0:T(8,128)} %get-tuple-element.132, f32[4,1024]{1,0:T(4,128)S(1)} %copy-done.137), kind=kLoop, calls=%fused_computation.8 | loop fusion | flops 33554432 | bytes 83918848 | tf_op jit(solution)/shard_map/convert_element_type | solution.py:188
  1887.3 25.2 %multiply_reduce_fusion = (f32[4,1024]{1,0:T(4,128)S(1)}, f32[4,1024,2048]{2,1,0:T(8,128)}) fusion(f32[4,1024,2048]{2,1,0:T(8,128)} %get-tuple-element.134, f32[4,1024]{1,0:T(4,128)S(1)} %copy-done.133, bf16[1024,4,72]{0,2,1:T(8,128)(2,1)S(1)} %bitcast.661, bf16[2048,4,72]{0,2,1:T(8,128)(2,1)} %bitcast.647), kind=kOutput, calls=%fused_computation.5 | convolution fusion | flops 1233121280 | bytes 68911104 | tf_op jit(solution)/shard_map/qhd,khd->hqk/dot_general | solution.py:184
  1918.9 28.3 %multiply_convert_fusion = bf16[4,1024,2048]{2,1,0:T(8,128)(2,1)} fusion(f32[4,1024,2048]{2,1,0:T(8,128)} %get-tuple-element.142, f32[4,1024]{1,0:T(4,128)S(1)} %get-tuple-element.141, f32[4,1024,2048]{2,1,0:T(8,128)} %get-tuple-element.134, f32[4,1024]{1,0:T(4,128)S(1)} %copy-done.133), kind=kLoop, calls=%fused_computation.4 | loop fusion | flops 33554432 | bytes 83918848 | tf_op jit(solution)/shard_map/convert_element_type | solution.py:188
  2117.1 31.8 %reduce-scatter.79.cloned.1.call-done = bf16[144,288]{1,0:T(8,128)(2,1)} async-done(((bf16[1152,288]{1,0:T(8,128)(2,1)}), bf16[144,288]{1,0:T(8,128)(2,1)}) %reduce-scatter.79.cloned.1.call-update) | async-done | bytes 82960 | tf_op jit(solution)/shard_map/reduce_scatter | solution.py:231
  2155.0 32.1 %reduce-scatter.83.cloned.1.call-done = bf16[144,288]{1,0:T(8,128)(2,1)} async-done(((bf16[1152,288]{1,0:T(8,128)(2,1)}), bf16[144,288]{1,0:T(8,128)(2,1)}) %reduce-scatter.83.cloned.1.call-update) | async-done | bytes 82960 | tf_op jit(solution)/shard_map/reduce_scatter | solution.py:237
  2188.7 37.0 %reduce-scatter.81.cloned.1.call-done = bf16[144,288]{1,0:T(8,128)(2,1)} async-done(((bf16[1152,288]{1,0:T(8,128)(2,1)}), bf16[144,288]{1,0:T(8,128)(2,1)}) %reduce-scatter.81.cloned.1.call-update) | async-done | bytes 82960 | tf_op jit(solution)/shard_map/reduce_scatter | solution.py:234
  2227.3 48.8 %reduce-scatter.53.cloned.1.call-done = bf16[256,1152]{1,0:T(8,128)(2,1)} async-done(((bf16[1024,1152]{1,0:T(8,128)(2,1)}), bf16[256,1152]{1,0:T(8,128)(2,1)}) %reduce-scatter.53.cloned.1.call-update) | async-done | bytes 589840 | tf_op jit(solution)/shard_map/reduce_scatter | solution.py:219
  2276.0 49.7 %reduce-scatter.61.cloned.1.call-done = bf16[256,1152]{1,0:T(8,128)(2,1)} async-done(((bf16[1024,1152]{1,0:T(8,128)(2,1)}), bf16[256,1152]{1,0:T(8,128)(2,1)}) %reduce-scatter.61.cloned.1.call-update) | async-done | bytes 589840 | tf_op jit(solution)/shard_map/reduce_scatter | solution.py:219
  2325.8 49.9 %reduce-scatter.77.cloned.1.call-done = bf16[256,1152]{1,0:T(8,128)(2,1)} async-done(((bf16[1024,1152]{1,0:T(8,128)(2,1)}), bf16[256,1152]{1,0:T(8,128)(2,1)}) %reduce-scatter.77.cloned.1.call-update) | async-done | bytes 589840 | tf_op jit(solution)/shard_map/reduce_scatter | solution.py:219
  2390.6 42.4 %all-reduce = (f32[1152]{0:T(1024)}, f32[1152]{0:T(1024)}, f32[1152]{0:T(1024)}, f32[1152]{0:T(1024)}, f32[1152]{0:T(1024)}, /*index=5*/f32[1152]{0:T(1024)}, f32[1152]{0:T(1024)}, f32[4304]{0:T(1024)}, f32[1152]{0:T(1024)}) all-reduce(f32[1152]{0:T(1024)S(1)} %copy-done.120, ...), channel_id=1, replica_groups=mesh['fsdp'=4,'ctx'=2,'tp'=4] {'fsdp','ctx','tp'}, use_global_device_ids=true, to_apply=%region_72.74 | all-reduce | flops 13520 | bytes 108160 | tf_op jit(solution)/shard_map/psum | solution.py:253
  (789 shorter events, 738.2 us)
Async XLA Ops:
  136.1 101.0 %all-gather.47.cloned.1.call-start = ((), (), s32[]{:S(2)}) async-start(), calls=%async_computation.42 | async-start | bytes 2949120 | tf_op jit(solution)/shard_map/all_gather | solution.py:94
  251.4 105.9 %reduce-scatter.39.cloned.1.call-start = ((), (), s32[]{:S(2)}) async-start(), calls=%async_computation.45 | async-start | bytes 2949120 | tf_op jit(solution)/shard_map/reduce_scatter | solution.py:130
  309.1 104.9 %all-gather.53.cloned.1.call-start = ((), (), s32[]{:S(2)}) async-start(), calls=%async_computation.47 | async-start | bytes 2949120 | tf_op jit(solution)/shard_map/all_gather | solution.py:94
  363.8 137.8 %all-gather.41.cloned.1.call-start = ((), (), s32[]{:S(2)}) async-start(), calls=%async_computation.37 | async-start | bytes 2949120 | tf_op jit(solution)/shard_map/all_gather | solution.py:94
  364.4 164.4 %all-gather.37.cloned.1.call-start = ((), (), s32[]{:S(2)}) async-start(), calls=%async_computation.34 | async-start | bytes 3317760 | tf_op jit(solution)/shard_map/all_gather | solution.py:61
  365.2 215.7 %all-gather.67.cloned.1.call-start = ((), (), s32[]{:S(2)}) async-start(), calls=%async_computation.78 | async-start | bytes 2949120 | tf_op jit(solution)/shard_map/all_gather | solution.py:138
  368.4 238.6 %all-gather.39.cloned.1.call-start = ((), (), s32[]{:S(2)}) async-start(), calls=%async_computation.35 | async-start | bytes 3317760 | tf_op jit(solution)/shard_map/all_gather | solution.py:62
  369.1 330.8 %all-gather.71.cloned.1.call-start = ((), (), s32[]{:S(2)}) async-start(), calls=%async_computation.80 | async-start | bytes 2949120 | tf_op jit(solution)/shard_map/all_gather | solution.py:138
  369.7 357.0 %all-gather.57.cloned.1.call-start = ((), (), s32[]{:S(2)}) async-start(), calls=%async_computation.49 | async-start | bytes 1769472 | tf_op jit(solution)/shard_map/all_gather | solution.py:100
  417.5 328.9 %all-gather.55.cloned.1.call-start = ((), (), s32[]{:S(2)}) async-start(), calls=%async_computation.48 | async-start | bytes 1769472 | tf_op jit(solution)/shard_map/all_gather | solution.py:101
  421.1 356.9 %all-gather.45.cloned.1.call-start = ((), (), s32[]{:S(2)}) async-start(), calls=%async_computation.39 | async-start | bytes 1769472 | tf_op jit(solution)/shard_map/all_gather | solution.py:100
  474.3 152.4 %collective-permute-start.6 = (bf16[256,1152]{1,0:T(8,128)(2,1)S(1)}, bf16[256,1152]{1,0:T(8,128)(2,1)}, u32[]{:S(2)}, u32[]{:S(2)}) collective-permute-start(bf16[256,1152]{1,0:T(8,128)(2,1)S(1)} %copy-done.53), channel_id=1, source_target_pairs={{0,1},{1,2},{2,3},{3,0},{4,5},{5,6},{6,7},{7,4},{8,9},{9,10},{10,1... | collective-permute-start | bytes 1769480 | tf_op jit(solution)/shard_map/ppermute | solution.py:18
  505.2 292.5 %all-gather.43.cloned.1.call-start = ((), (), s32[]{:S(2)}) async-start(), calls=%async_computation.38 | async-start | bytes 1769472 | tf_op jit(solution)/shard_map/all_gather | solution.py:101
  538.5 296.9 %reduce-scatter.47.cloned.1.call-start = ((), (), s32[]{:S(2)}) async-start(), calls=%async_computation.52 | async-start | bytes 2949120 | tf_op jit(solution)/shard_map/reduce_scatter | solution.py:157
  623.2 257.6 %reduce-scatter.63.cloned.1.call-start = ((), (), s32[]{:S(2)}) async-start(), calls=%async_computation.62 | async-start | bytes 2949120 | tf_op jit(solution)/shard_map/reduce_scatter | solution.py:157
  716.2 214.5 %reduce-scatter.43.cloned.1.call-start = ((), (), s32[]{:S(2)}) async-start(), calls=%async_computation.50 | async-start | bytes 2949120 | tf_op jit(solution)/shard_map/reduce_scatter | solution.py:130
  767.4 213.2 %reduce-scatter.35.cloned.1.call-start = ((), (), s32[]{:S(2)}) async-start(), calls=%async_computation.40 | async-start | bytes 2949120 | tf_op jit(solution)/shard_map/reduce_scatter | solution.py:130
  816.9 213.5 %reduce-scatter.41.cloned.1.call-start = ((), (), s32[]{:S(2)}) async-start(), calls=%async_computation.46 | async-start | bytes 2949120 | tf_op jit(solution)/shard_map/reduce_scatter | solution.py:143
  826.2 253.9 %reduce-scatter.33.cloned.1.call-start = ((), (), s32[]{:S(2)}) async-start(), calls=%async_computation.36 | async-start | bytes 2949120 | tf_op jit(solution)/shard_map/reduce_scatter | solution.py:143
  835.3 306.8 %all-gather.63.cloned.1.call-start = ((), (), s32[]{:S(2)}) async-start(), calls=%async_computation.63 | async-start | bytes 2949120 | tf_op jit(solution)/shard_map/all_gather | solution.py:173
  1037.0 260.6 %all-gather.73.cloned.1.call-start = ((), (), s32[]{:S(2)}) async-start(), calls=%async_computation.81 | async-start | bytes 2949120 | tf_op jit(solution)/shard_map/all_gather | solution.py:138
  1037.6 330.1 %all-gather.69.cloned.1.call-start = ((), (), s32[]{:S(2)}) async-start(), calls=%async_computation.79 | async-start | bytes 2949120 | tf_op jit(solution)/shard_map/all_gather | solution.py:138
  1038.2 361.8 %reduce-scatter.65.cloned.1.call-start = ((), (), s32[]{:S(2)}) async-start(), calls=%async_computation.64 | async-start | bytes 1769472 | tf_op jit(solution)/shard_map/reduce_scatter | solution.py:202
  1086.4 119.1 %collective-permute-start.9 = (bf16[256,1152]{1,0:T(8,128)(2,1)}, bf16[256,1152]{1,0:T(8,128)(2,1)S(1)}, u32[]{:S(2)}, u32[]{:S(2)}) collective-permute-start(bf16[256,1152]{1,0:T(8,128)(2,1)} %get-tuple-element.106), channel_id=1, source_target_pairs={{0,1},{1,2},{2,3},{3,0},{4,5},{5,6},{6,7},{7,4},{8,9},{9,10},{10,1... | collective-permute-start | bytes 1769480 | tf_op jit(solution)/shard_map/ppermute | solution.py:18
  1205.4 201.0 %reduce-scatter.67.cloned.1.call-start = ((), (), s32[]{:S(2)}) async-start(), calls=%async_computation.65 | async-start | bytes 1769472 | tf_op jit(solution)/shard_map/reduce_scatter | solution.py:205
  1207.5 106.6 %collective-permute-start.3 = (bf16[256,1152]{1,0:T(8,128)(2,1)S(1)}, bf16[256,1152]{1,0:T(8,128)(2,1)S(1)}, u32[]{:S(2)}, u32[]{:S(2)}) collective-permute-start(bf16[256,1152]{1,0:T(8,128)(2,1)S(1)} %copy-done.59), channel_id=1, source_target_pairs={{0,1},{1,2},{2,3},{3,0},{4,5},{5,6},{6,7},{7,4},{8,9},{9,10},{10,1... | collective-permute-start | bytes 1769480 | tf_op jit(solution)/shard_map/ppermute | solution.py:18
  1289.5 141.4 %reduce-scatter.71.cloned.1.call-start = ((), (), s32[]{:S(2)}) async-start(), calls=%async_computation.67 | async-start | bytes 2949120 | tf_op jit(solution)/shard_map/reduce_scatter | solution.py:157
  1314.0 116.9 %reduce-scatter.55.cloned.1.call-start = ((), (), s32[]{:S(2)}) async-start(), calls=%async_computation.57 | async-start | bytes 2949120 | tf_op jit(solution)/shard_map/reduce_scatter | solution.py:157
  1412.1 118.1 %reduce-scatter.37.cloned.1.call-start = ((), (), s32[]{:S(2)}) async-start(), calls=%async_computation.41 | async-start | bytes 2949120 | tf_op jit(solution)/shard_map/reduce_scatter | solution.py:143
  1420.5 160.1 %reduce-scatter.45.cloned.1.call-start = ((), (), s32[]{:S(2)}) async-start(), calls=%async_computation.51 | async-start | bytes 2949120 | tf_op jit(solution)/shard_map/reduce_scatter | solution.py:143
  1429.5 208.3 %all-gather.59.cloned.1.call-start = ((), (), s32[]{:S(2)}) async-start(), calls=%async_computation.53 | async-start | bytes 2949120 | tf_op jit(solution)/shard_map/all_gather | solution.py:173
  1587.7 100.9 %all-gather.65.cloned.1.call-start = ((), (), s32[]{:S(2)}) async-start(), calls=%async_computation.68 | async-start | bytes 2949120 | tf_op jit(solution)/shard_map/all_gather | solution.py:173
  1588.2 151.6 %all-gather.61.cloned.1.call-start = ((), (), s32[]{:S(2)}) async-start(), calls=%async_computation.58 | async-start | bytes 2949120 | tf_op jit(solution)/shard_map/all_gather | solution.py:173
  1588.8 462.0 %reduce-scatter.51.cloned.1.call-start = ((), (), s32[]{:S(2)}) async-start(), calls=%async_computation.55 | async-start | bytes 1769472 | tf_op jit(solution)/shard_map/reduce_scatter | solution.py:205
  1657.1 398.2 %reduce-scatter.59.cloned.1.call-start = ((), (), s32[]{:S(2)}) async-start(), calls=%async_computation.60 | async-start | bytes 1769472 | tf_op jit(solution)/shard_map/reduce_scatter | solution.py:205
  1776.8 285.1 %reduce-scatter.75.cloned.1.call-start = ((), (), s32[]{:S(2)}) async-start(), calls=%async_computation.70 | async-start | bytes 1769472 | tf_op jit(solution)/shard_map/reduce_scatter | solution.py:205
  1798.9 267.9 %reduce-scatter.49.cloned.1.call-start = ((), (), s32[]{:S(2)}) async-start(), calls=%async_computation.54 | async-start | bytes 1769472 | tf_op jit(solution)/shard_map/reduce_scatter | solution.py:202
  1858.9 212.4 %reduce-scatter.57.cloned.1.call-start = ((), (), s32[]{:S(2)}) async-start(), calls=%async_computation.59 | async-start | bytes 1769472 | tf_op jit(solution)/shard_map/reduce_scatter | solution.py:202
  1918.8 159.2 %reduce-scatter.73.cloned.1.call-start = ((), (), s32[]{:S(2)}) async-start(), calls=%async_computation.69 | async-start | bytes 1769472 | tf_op jit(solution)/shard_map/reduce_scatter | solution.py:202
  1957.0 149.1 %reduce-scatter.89.cloned.1.call-start = ((), (), s32[]{:S(2)}) async-start(), calls=%async_computation.77 | async-start | bytes 2985984 | tf_op jit(solution)/shard_map/reduce_scatter | solution.py:246
  1976.6 131.4 %reduce-scatter.87.cloned.1.call-start = ((), (), s32[]{:S(2)}) async-start(), calls=%async_computation.76 | async-start | bytes 2985984 | tf_op jit(solution)/shard_map/reduce_scatter | solution.py:243
  1994.9 120.4 %reduce-scatter.85.cloned.1.call-start = ((), (), s32[]{:S(2)}) async-start(), calls=%async_computation.75 | async-start | bytes 995328 | tf_op jit(solution)/shard_map/reduce_scatter | solution.py:240
  2041.1 107.8 %reduce-scatter.79.cloned.1.call-start = ((), (), s32[]{:S(2)}) async-start(), calls=%async_computation.72 | async-start | bytes 995328 | tf_op jit(solution)/shard_map/reduce_scatter | solution.py:231
  2050.4 136.7 %reduce-scatter.83.cloned.1.call-start = ((), (), s32[]{:S(2)}) async-start(), calls=%async_computation.74 | async-start | bytes 995328 | tf_op jit(solution)/shard_map/reduce_scatter | solution.py:237
  2066.8 158.9 %reduce-scatter.81.cloned.1.call-start = ((), (), s32[]{:S(2)}) async-start(), calls=%async_computation.73 | async-start | bytes 995328 | tf_op jit(solution)/shard_map/reduce_scatter | solution.py:234
  2082.9 193.2 %reduce-scatter.53.cloned.1.call-start = ((), (), s32[]{:S(2)}) async-start(), calls=%async_computation.56 | async-start | bytes 2949120 | tf_op jit(solution)/shard_map/reduce_scatter | solution.py:219
  2089.3 236.5 %reduce-scatter.61.cloned.1.call-start = ((), (), s32[]{:S(2)}) async-start(), calls=%async_computation.61 | async-start | bytes 2949120 | tf_op jit(solution)/shard_map/reduce_scatter | solution.py:219
  2096.7 279.0 %reduce-scatter.77.cloned.1.call-start = ((), (), s32[]{:S(2)}) async-start(), calls=%async_computation.71 | async-start | bytes 2949120 | tf_op jit(solution)/shard_map/reduce_scatter | solution.py:219
  (243 other events, 7199.3 us)
Sparse Core Ops, SparseCore 0:
  11.2 53.1 all-gather.30
  68.2 21.5 all-gather.34
  92.0 22.7 all-gather.32
  136.3 48.0 reduce-scatter.30
  187.1 49.9 all-gather.46
  241.0 21.5 all-gather.50
  264.7 22.7 all-gather.48
  309.2 48.0 reduce-scatter.38
  364.0 49.9 all-gather.52
  416.0 85.6 all-gather.40
  503.2 25.6 all-gather.36
  530.3 50.4 all-gather.66
  582.4 24.5 all-gather.38
  608.4 75.3 all-gather.70
  685.2 21.5 all-gather.56
  708.2 22.8 all-gather.54
  732.5 22.7 all-gather.44
  756.7 22.8 all-gather.42
  782.5 48.0 reduce-scatter.46
  833.2 47.5 reduce-scatter.62
  883.1 47.5 reduce-scatter.42
  933.0 47.5 reduce-scatter.34
  982.9 47.5 reduce-scatter.40
  1032.6 47.5 reduce-scatter.32
  1081.7 60.2 all-gather.62
  1143.5 49.0 all-gather.72
  1194.0 83.6 all-gather.68
  1279.9 21.4 reduce-scatter.64
  1303.7 21.7 reduce-scatter.66
  1327.6 52.3 reduce-scatter.70
  1384.0 46.4 reduce-scatter.54
  1432.9 47.5 reduce-scatter.68
  1482.6 47.5 reduce-scatter.36
  1533.0 47.5 reduce-scatter.44
  1587.8 49.9 all-gather.58
  1639.2 49.2 all-gather.64
  1690.5 49.2 all-gather.60
  1777.0 20.5 reduce-scatter.58
  1799.8 21.7 reduce-scatter.74
  1980.2 43.7 reduce-scatter.88
  2028.3 43.7 reduce-scatter.86
  2075.1 35.1 reduce-scatter.84
  2113.7 35.0 reduce-scatter.78
  2151.9 35.1 reduce-scatter.82
  2190.5 35.0 reduce-scatter.80
  2228.0 48.0 reduce-scatter.52
  2278.2 47.5 reduce-scatter.60
  2328.1 47.5 reduce-scatter.76
  (4 shorter events, 79.2 us)
